TPU v7x, 512 devices: a whole 4x4x16 slice. The times are simulated.
512 devices in a mesh: sec: 8 (over x, core), xy: 64 (over y, z).
Axes of the slice: x: 4, y: 4, z: 16, core: 2. Of those that a mesh axis runs over, the one named last changes fastest.
Arguments:
- source: bfloat16 [8, 32768, 1024], P('sec', 'xy'), may hold values from -6 to 6
- coarse: int32 [8, 2, 128], P('sec', None, 'xy'), may hold values from -1 to 1, as said below
- fraction: float32 [8, 2, 128], P('sec', None, 'xy'), may hold values from 0.25 to 0.75
- kernel_one: float32 [3, 3, 3], replicated, may hold values from -1.25 to 1.25
- kernel_two: float32 [3, 3, 3], replicated, may hold values from -1.25 to 1.25
Outputs:
- denoised: bfloat16 [8, 1024, 32768], P(None, 'xy', 'sec')
Inputs may be any that keep to these rules, and one draw needn't show every extreme that they name: Destination block (r, c) reads source block (r + coarse[z, 0, b], c + coarse[z, 1, b]); c + coarse[z, 1, b] always lies in 0 to 1. Among the 2 blocks of one block row of a section, at most one has a row offset of -1 and at most one has +1.
All inputs are finite; a program needn't handle non-finite values.
Results may differ from a plain program's by a relative error of at most 0.003.
The roundings to bfloat16 on the way count: a program that leaves them out, or rounds other values in their place, can miss the bound.
Values may be sent and summed in bfloat16 or wider, within the bound.
No kernel may reach another device: no remote copies, remote signals or barrier semaphores. Data moves between devices by JAX's collectives and lax.ppermute only.
A program may use at most 128 MiB of HBM per device.

v0:
```python
import jax
import jax.numpy as jnp
from jax import lax
from jax.sharding import PartitionSpec as P


def from_behind(value, axis, steps):
    count = lax.axis_size(axis)
    first, last = (max(0, -steps), min(count, count - steps))
    return lax.ppermute(value, axis, [(source, source + steps) for source in range(first, last)])


def with_halo(x, sides, width):
    for axis, dim in sides:
        size, length = (lax.axis_size(axis), x.shape[dim])
        up = [(i, (i + 1) % size) for i in range(size - 1)]
        down = [(j, i) for i, j in up]
        last = lax.slice_in_dim(x, length - width, length, axis=dim)
        first = lax.slice_in_dim(x, 0, width, axis=dim)
        before = lax.ppermute(last, axis, up)
        after = lax.ppermute(first, axis, down)
        x = jnp.concatenate([before, x, after], axis=dim)
    return x


def interpolation(shift, edge):
    row_index = lax.broadcasted_iota(jnp.int32, (edge, edge), 0)
    col_index = lax.broadcasted_iota(jnp.int32, (edge, edge), 1)
    offset = col_index - row_index
    amount = shift[..., None, None]
    w_before = ((-0.5 * amount + 1.0) * amount - 0.5) * amount
    w_center = (1.5 * amount - 2.5) * amount * amount + 1.0
    w_after = ((-1.5 * amount + 2.0) * amount + 0.5) * amount
    w_beyond = (0.5 * amount - 0.5) * amount * amount
    matrix = jnp.where(offset == -1, w_before, 0.0) + jnp.where(offset == 0, w_center, 0.0)
    matrix = matrix + jnp.where(offset == 1, w_after, 0.0) + jnp.where(offset == 2, w_beyond, 0.0)
    return matrix.astype(jnp.bfloat16)


def pad_sections(volume):
    return jnp.pad(volume, ((1, 1), (0, 0), (0, 0)))


def stencil(padded, kernel, depth, cols_out, rows_out):
    running = jnp.zeros((depth, cols_out, rows_out), jnp.float32)
    for tap_z in range(3):
        for tap_x in range(3):
            for tap_y in range(3):
                window = padded[
                    tap_z : tap_z + depth, tap_x : tap_x + cols_out, tap_y : tap_y + rows_out
                ]
                running = running + kernel[tap_z, tap_x, tap_y] * window
    return running


def body(source, coarse, fraction, kernel_one, kernel_two):
    sections_dev, edge, width = source.shape
    columns = width // edge
    row_shift = coarse[:, 0, :]
    col_shift = coarse[:, 1, :]
    target = lax.broadcasted_iota(jnp.int32, (sections_dev, columns, columns), 1)
    anchor = lax.broadcasted_iota(jnp.int32, (sections_dev, columns, columns), 2)
    from_above = from_behind(source, "xy", 1)
    from_below = from_behind(source, "xy", -1)
    stacked = jnp.stack([from_above, source, from_below]).reshape(
        3, sections_dev, edge, columns, edge
    )
    level = lax.broadcasted_iota(jnp.int32, (3, sections_dev, columns, columns), 0)
    choose = (row_shift[None, :, :, None] + 1 == level) & (
        target[None] + col_shift[None, :, :, None] == anchor[None]
    )
    picked = jnp.einsum(
        "ksnm,ksimj->snij", choose.astype(jnp.bfloat16), stacked, preferred_element_type=jnp.float32
    ).astype(jnp.bfloat16)
    row_matrix = interpolation(fraction[:, 0, :], edge)
    col_matrix = interpolation(fraction[:, 1, :], edge)
    rows_warped = jnp.einsum(
        "snij,snjk->snik", row_matrix, picked, preferred_element_type=jnp.float32
    ).astype(jnp.bfloat16)
    warped = jnp.einsum(
        "sncj,snrj->sncr", col_matrix, rows_warped, preferred_element_type=jnp.float32
    ).astype(jnp.bfloat16)
    aligned_strip = warped.reshape(sections_dev, width, edge)
    group_data = lax.all_to_all(
        lax.all_to_all(aligned_strip, "xy", split_axis=1, concat_axis=2, tiled=True),
        "sec",
        split_axis=2,
        concat_axis=0,
        tiled=True,
    )
    sections_all, group_cols, group_rows = group_data.shape
    rim_one = with_halo(group_data, (("sec", 2), ("xy", 1)), 1)
    first_pass = jnp.maximum(
        stencil(
            pad_sections(rim_one.astype(jnp.float32)),
            kernel_one,
            sections_all,
            group_cols,
            group_rows,
        ),
        0.0,
    ).astype(jnp.bfloat16)
    rim_two = with_halo(first_pass, (("sec", 2), ("xy", 1)), 1)
    second = stencil(
        pad_sections(rim_two.astype(jnp.float32)), kernel_two, sections_all, group_cols, group_rows
    )
    return (second + group_data.astype(jnp.float32)).astype(jnp.bfloat16)


def solution(mesh):
    placed = (P("sec", "xy", None), P("sec", None, "xy"), P("sec", None, "xy"), P(), P())
    return jax.shard_map(
        body, mesh=mesh, in_specs=placed, out_specs=P(None, "xy", "sec"), check_vma=False
    )
```

profile of v0, /device:TPU:9, one launch (start us, length us, event | category | flops | bytes accessed | tf_op | source)
XLA Modules:
  0.0 503.7 jit_solution(17445958585612541648)
XLA Ops:
  0.0 3.7 collective-permute-start
  3.7 9.4 %collective-permute-start.1 = (bf16[1,512,1024]{2,1,0:T(8,128)(2,1)}, bf16[1,512,1024]{2,1,0:T(8,128)(2,1)S(1)}, u32[]{:S(2)}, u32[]{:S(2)}) collective-permute-start(bf16[1,512,1024]{2,1,0:T(8,128)(2,1)} %param.5), channel_id=1, source_target_pairs={{1,0},{2,1},{3,2},{4,3},{5,4},{6,5},{7,6},{8,7},{9,8},{10,9},{11,1... | collective-permute-start | bytes 3145736 | tf_op jit(solution)/shard_map/ppermute | solution.py:10
  13.1 0.9 fusion.109
  13.9 1.8 stack.13
  15.8 1.0 fusion.111
  16.8 0.0 copy-done.8
  16.8 0.1 iota_compare_fusion.1
  16.8 0.1 fusion.122
  16.9 0.0 copy-done.7
  16.9 17.3 %collective-permute-done = bf16[1,512,1024]{2,1,0:T(8,128)(2,1)S(1)} collective-permute-done((bf16[1,512,1024]{2,1,0:T(8,128)(2,1)}, bf16[1,512,1024]{2,1,0:T(8,128)(2,1)S(1)}, u32[]{:S(2)}, u32[]{:S(2)}) %collective-permute-start) | collective-permute-done | bytes 1048608 | tf_op jit(solution)/shard_map/ppermute | solution.py:10
  34.2 1.6 stack.12
  35.8 0.0 collective-permute-done.1
  35.8 0.8 stack.14
  36.6 8.0 %bitcast_convert_fusion = bf16[2,512,512]{2,0,1:T(2,128)(2,1)} fusion(bf16[1,1,512,2,512]{4,3,0,2,1:T(2,128)(2,1)S(1)} %stack.14, bf16[1,1,512,2,512]{4,3,0,2,1:T(2,128)(2,1)S(1)} %stack.13, bf16[1,1,512,2,512]{4,3,0,2,1:T(2,128)(2,1)} %stack.12, pred[3,2,2]{2,0,1:T(4,128)(4,1)S(1)} %fusion.122), kind=kOutput, calls=%fused_computation.148 | convolution fusion | flops 16252928 | bytes 4194316 | tf_op jit(solution)/shard_map/ksnm,ksimj->snij/dot_general | solution.py:72
  44.6 3.9 convolution_convert_fusion
  48.5 1.6 copy.28
  50.1 0.5 broadcast.323
  50.7 7.0 %reduce = bf16[1024,512]{1,0:T(8,128)(2,1)S(1)} reduce(bf16[1024,1,512]{2,1,0:T(2,128)(2,1)S(1)} %bitcast.173, bf16[]{:T(256)} %broadcast.323), dimensions={1}, to_apply=%bitcast.165.reduce_sub_computation | reduce | bytes 2097154
  57.7 0.8 reshape.317
  58.5 60.3 %all_to_all.36 = bf16[64,2,4096]{2,1,0:T(2,128)(2,1)S(1)} all-to-all(bf16[64,2,4096]{2,1,0:T(2,128)(2,1)S(1)} %reshape.317), channel_id=1, replica_groups=mesh['sec'=8,'xy'=64] {'xy'}, dimensions={0} | all-to-all | bytes 2097152 | tf_op jit(solution)/shard_map/all_to_all | solution.py:85
  118.8 1.0 reshape.318
  119.8 0.3 copy.19
  120.1 0.1 copy.20
  120.2 25.0 %copy.15 = bf16[1,16,32768]{1,0,2:T(2,128)(2,1)} copy(bf16[1,16,32768]{2,1,0:T(8,128)(2,1)S(1)} %bitcast.175) | data formatting | bytes 2097152 | tf_op jit(solution)/shard_map/all_to_all | solution.py:85
  145.2 179.2 %reduce.1 = bf16[32768,16]{1,0:T(8,128)(2,1)} reduce(bf16[32768,1,16]{2,1,0:T(2,128)(2,1)} %bitcast.168, bf16[]{:T(256)} %broadcast.323), dimensions={1}, to_apply=%bitcast.162.reduce_sub_computation | reduce | bytes 2097154
  324.4 10.4 %reshape.319 = bf16[8,2,32768]{2,1,0:T(2,128)(2,1)S(1)} reshape(bf16[32768,16]{1,0:T(8,128)(2,1)} %reduce.1) | data formatting | bytes 2097152
  334.8 25.2 %all_to_all.37 = bf16[8,2,32768]{2,1,0:T(2,128)(2,1)S(1)} all-to-all(bf16[8,2,32768]{2,1,0:T(2,128)(2,1)S(1)} %reshape.319), channel_id=1, replica_groups=mesh['sec'=8,'xy'=64] {'sec'}, dimensions={0} | all-to-all | bytes 2097152 | tf_op jit(solution)/shard_map/all_to_all | solution.py:84
  360.0 12.2 %reshape.320 = bf16[32768,1,16]{2,1,0:T(2,128)(2,1)} reshape(bf16[8,2,32768]{2,1,0:T(2,128)(2,1)S(1)} %all_to_all.37) | data formatting | bytes 2097152
  372.3 29.6 %copy.16 = bf16[1,16,32768]{2,1,0:T(8,128)(2,1)S(1)} copy(bf16[1,16,32768]{1,0,2:T(2,128)(2,1)} %bitcast.169) | data formatting | bytes 2097152 | tf_op jit(solution)/shard_map/all_to_all | solution.py:84
  401.9 0.0 copy-start.5
  402.0 0.6 copy.21
  402.5 0.1 bitcast_bitcast_fusion
  402.6 0.1 fusion.143
  402.7 3.1 collective-permute-start.2
  405.8 1.9 collective-permute-start.3
  407.8 0.7 fusion.146
  408.5 0.0 collective-permute-done.2
  408.5 2.6 collective-permute-done.3
  411.1 1.6 concatenate.13
  412.7 0.0 copy-start
  412.7 3.1 collective-permute-start.4
  415.8 4.6 collective-permute-start.5
  420.4 0.7 fusion.147
  421.1 0.0 collective-permute-done.4
  421.1 0.4 collective-permute-done.5
  421.4 1.4 maximum_convert_fusion
  422.9 0.0 copy-start.6
  422.9 27.6 %fusion.43 = bf16[8,16,4096]{2,0,1:T(8,128)(2,1)} fusion(f32[8,18,4098]{2,0,1:T(8,128)S(1)} %maximum_convert_fusion, f32[]{:T(128)} %bitcast.41, f32[]{:T(128)} %bitcast.40, f32[]{:T(128)} %bitcast.39, f32[]{:T(128)} %bitcast.38, f32[]{:T(128)} %bitcast.37, f32[]{:T(128)} %bitcast.36, f32[]{:T(128)} %bitcast.35, f32[]{:T(128)} %bitcast.34, f32[]{:T(128)} %bitcast.33, ...), kind=kLoop, calls=%fused_computation.80 | loop fusion | flops 28835840 | bytes 22356076 | tf_op jit(solution)/shard_map/convert_element_type | solution.py:102
  450.5 0.9 fusion.142
  451.3 3.0 collective-permute-start.6
  454.3 1.9 collective-permute-start.7
  456.3 0.7 fusion.144
  457.0 0.0 collective-permute-done.6
  457.0 2.6 collective-permute-done.7
  459.6 2.9 concatenate.15
  462.5 0.0 copy-start.1
  462.5 2.3 collective-permute-start.8
  464.8 5.7 %collective-permute-start.9 = (bf16[8,1,4098]{2,0,1:T(8,128)(2,1)S(1)}, bf16[8,1,4098]{2,0,1:T(8,128)(2,1)S(1)}, u32[]{:S(2)}, u32[]{:S(2)}) collective-permute-start(bf16[8,1,4098]{2,0,1:T(8,128)(2,1)S(1)} %get-tuple-element.6), channel_id=1, source_target_pairs={{1,0},{2,1},{3,2},{4,3},{5,4},{6,5},{7,6},{8,7},{9,8},{10,9},{11,1... | collective-permute-start | bytes 196712 | tf_op jit(solution)/shard_map/ppermute | solution.py:21
  470.5 0.7 fusion.145
  471.2 0.0 collective-permute-done.8
  471.2 0.6 collective-permute-done.9
  471.9 1.4 maximum_convert_fusion.1
  473.3 27.6 %fusion.89 = bf16[8,16,4096]{2,0,1:T(8,128)(2,1)} fusion(f32[8,18,4098]{2,0,1:T(8,128)S(1)} %maximum_convert_fusion.1, f32[]{:T(128)} %bitcast.67, f32[]{:T(128)} %bitcast.66, f32[]{:T(128)} %bitcast.65, f32[]{:T(128)} %bitcast.64, f32[]{:T(128)} %bitcast.63, f32[]{:T(128)} %bitcast.62, f32[]{:T(128)} %bitcast.61, f32[]{:T(128)} %bitcast.60, f32[]{:T(128)} %bitcast.59, ...), kind=kLoop, calls=%fused_computation.126 | loop fusion | flops 29360128 | bytes 23404652 | tf_op jit(solution)/shard_map/convert_element_type | solution.py:107
  500.9 2.8 copy.17
  (16 shorter events, 0.1 us)
Async XLA Ops:
  0.0 16.8 %copy-start.8 = (s32[1,2,2]{2,1,0:T(2,128)S(1)}, s32[1,2,2]{2,1,0:T(2,128)}, u32[]{:S(2)}) copy-start(s32[1,2,2]{2,1,0:T(2,128)} %param.6) | copy-start | bytes 52
  0.0 16.9 %copy-start.7 = (f32[1,2,2]{2,1,0:T(2,128)S(1)}, f32[1,2,2]{2,1,0:T(2,128)}, u32[]{:S(2)}) copy-start(f32[1,2,2]{2,1,0:T(2,128)} %param.7) | copy-start | bytes 52
  0.0 34.2 %collective-permute-start = (bf16[1,512,1024]{2,1,0:T(8,128)(2,1)}, bf16[1,512,1024]{2,1,0:T(8,128)(2,1)S(1)}, u32[]{:S(2)}, u32[]{:S(2)}) collective-permute-start(bf16[1,512,1024]{2,1,0:T(8,128)(2,1)} %param.5), channel_id=1, source_target_pairs={{0,1},{1,2},{2,3},{3,4},{4,5},{5,6},{6,7},{7,8},{8,9},{9,10},{10,1... | collective-permute-start | bytes 3145736 | tf_op jit(solution)/shard_map/ppermute | solution.py:10
  3.7 32.1 %collective-permute-start.1 = (bf16[1,512,1024]{2,1,0:T(8,128)(2,1)}, bf16[1,512,1024]{2,1,0:T(8,128)(2,1)S(1)}, u32[]{:S(2)}, u32[]{:S(2)}) collective-permute-start(bf16[1,512,1024]{2,1,0:T(8,128)(2,1)} %param.5), channel_id=1, source_target_pairs={{1,0},{2,1},{3,2},{4,3},{5,4},{6,5},{7,6},{8,7},{9,8},{10,9},{11,1... | collective-permute-start | bytes 3145736 | tf_op jit(solution)/shard_map/ppermute | solution.py:10
  36.6 8.0 %copy-start.2 = (pred[512,512]{1,0:T(8,128)(4,1)S(1)}, pred[512,512]{1,0:T(8,128)(4,1)}, u32[]{:S(2)}) copy-start(pred[512,512]{1,0:T(8,128)(4,1)} %get-tuple-element.78) | copy-start | bytes 786436
  36.6 8.0 %copy-start.3 = (pred[512,512]{1,0:T(8,128)(4,1)S(1)}, pred[512,512]{1,0:T(8,128)(4,1)}, u32[]{:S(2)}) copy-start(pred[512,512]{1,0:T(8,128)(4,1)} %get-tuple-element.79) | copy-start | bytes 786436
  36.6 8.0 %copy-start.4 = (pred[512,512]{1,0:T(8,128)(4,1)S(1)}, pred[512,512]{1,0:T(8,128)(4,1)}, u32[]{:S(2)}) copy-start(pred[512,512]{1,0:T(8,128)(4,1)} %get-tuple-element.80) | copy-start | bytes 786436
  401.9 5.8 %copy-start.5 = (f32[3,3,3]{2,1,0:T(4,128)S(1)}, f32[3,3,3]{2,1,0:T(4,128)}, u32[]{:S(2)}) copy-start(f32[3,3,3]{2,1,0:T(4,128)} %param.8) | copy-start | bytes 328
  402.7 5.8 %collective-permute-start.2 = (bf16[8,16,1]{2,0,1:T(8,128)(2,1)S(1)}, bf16[8,16,1]{2,0,1:T(8,128)(2,1)S(1)}, u32[]{:S(2)}, u32[]{:S(2)}) collective-permute-start(bf16[8,16,1]{2,0,1:T(8,128)(2,1)S(1)} %get-tuple-element.12), channel_id=1, source_target_pairs={{0,64},{64,128},{128,192},{192,256},{256,320},{320,384},{384,448},... | collective-permute-start | bytes 776 | tf_op jit(solution)/shard_map/ppermute | solution.py:20
  405.8 5.2 %collective-permute-start.3 = (bf16[8,16,1]{2,0,1:T(8,128)(2,1)S(1)}, bf16[8,16,1]{2,0,1:T(8,128)(2,1)S(1)}, u32[]{:S(2)}, u32[]{:S(2)}) collective-permute-start(bf16[8,16,1]{2,0,1:T(8,128)(2,1)S(1)} %get-tuple-element.11), channel_id=1, source_target_pairs={{64,0},{128,64},{192,128},{256,192},{320,256},{384,320},{448,384},... | collective-permute-start | bytes 776 | tf_op jit(solution)/shard_map/ppermute | solution.py:21
  412.7 8.4 %copy-start = (bf16[8,16,4098]{2,0,1:T(8,128)(2,1)}, bf16[8,16,4098]{2,0,1:T(8,128)(2,1)S(1)}, u32[]{:S(2)}) copy-start(bf16[8,16,4098]{2,0,1:T(8,128)(2,1)S(1)} %concatenate.13) | copy-start | bytes 3147268
  412.7 8.4 %collective-permute-start.4 = (bf16[8,1,4098]{2,0,1:T(8,128)(2,1)S(1)}, bf16[8,1,4098]{2,0,1:T(8,128)(2,1)S(1)}, u32[]{:S(2)}, u32[]{:S(2)}) collective-permute-start(bf16[8,1,4098]{2,0,1:T(8,128)(2,1)S(1)} %get-tuple-element.7), channel_id=1, source_target_pairs={{0,1},{1,2},{2,3},{3,4},{4,5},{5,6},{6,7},{7,8},{8,9},{9,10},{10,1... | collective-permute-start | bytes 196712 | tf_op jit(solution)/shard_map/ppermute | solution.py:20
  415.8 5.7 %collective-permute-start.5 = (bf16[8,1,4098]{2,0,1:T(8,128)(2,1)S(1)}, bf16[8,1,4098]{2,0,1:T(8,128)(2,1)S(1)}, u32[]{:S(2)}, u32[]{:S(2)}) collective-permute-start(bf16[8,1,4098]{2,0,1:T(8,128)(2,1)S(1)} %get-tuple-element.8), channel_id=1, source_target_pairs={{1,0},{2,1},{3,2},{4,3},{5,4},{6,5},{7,6},{8,7},{9,8},{10,9},{11,1... | collective-permute-start | bytes 196712 | tf_op jit(solution)/shard_map/ppermute | solution.py:21
  422.9 33.4 %copy-start.6 = (f32[3,3,3]{2,1,0:T(4,128)S(1)}, f32[3,3,3]{2,1,0:T(4,128)}, u32[]{:S(2)}) copy-start(f32[3,3,3]{2,1,0:T(4,128)} %param.9) | copy-start | bytes 328
  451.3 5.7 %collective-permute-start.6 = (bf16[8,16,1]{2,0,1:T(8,128)(2,1)S(1)}, bf16[8,16,1]{2,0,1:T(8,128)(2,1)S(1)}, u32[]{:S(2)}, u32[]{:S(2)}) collective-permute-start(bf16[8,16,1]{2,0,1:T(8,128)(2,1)S(1)} %get-tuple-element.10), channel_id=1, source_target_pairs={{0,64},{64,128},{128,192},{192,256},{256,320},{320,384},{384,448},... | collective-permute-start | bytes 776 | tf_op jit(solution)/shard_map/ppermute | solution.py:20
  454.3 5.2 %collective-permute-start.7 = (bf16[8,16,1]{2,0,1:T(8,128)(2,1)S(1)}, bf16[8,16,1]{2,0,1:T(8,128)(2,1)S(1)}, u32[]{:S(2)}, u32[]{:S(2)}) collective-permute-start(bf16[8,16,1]{2,0,1:T(8,128)(2,1)S(1)} %get-tuple-element.9), channel_id=1, source_target_pairs={{64,0},{128,64},{192,128},{256,192},{320,256},{384,320},{448,384},... | collective-permute-start | bytes 776 | tf_op jit(solution)/shard_map/ppermute | solution.py:21
  462.5 8.7 %copy-start.1 = (bf16[8,16,4098]{2,0,1:T(8,128)(2,1)}, bf16[8,16,4098]{2,0,1:T(8,128)(2,1)S(1)}, u32[]{:S(2)}) copy-start(bf16[8,16,4098]{2,0,1:T(8,128)(2,1)S(1)} %concatenate.15) | copy-start | bytes 3147268
  462.5 8.7 %collective-permute-start.8 = (bf16[8,1,4098]{2,0,1:T(8,128)(2,1)S(1)}, bf16[8,1,4098]{2,0,1:T(8,128)(2,1)S(1)}, u32[]{:S(2)}, u32[]{:S(2)}) collective-permute-start(bf16[8,1,4098]{2,0,1:T(8,128)(2,1)S(1)} %get-tuple-element.5), channel_id=1, source_target_pairs={{0,1},{1,2},{2,3},{3,4},{4,5},{5,6},{6,7},{7,8},{8,9},{9,10},{10,1... | collective-permute-start | bytes 196712 | tf_op jit(solution)/shard_map/ppermute | solution.py:20
  464.8 7.0 %collective-permute-start.9 = (bf16[8,1,4098]{2,0,1:T(8,128)(2,1)S(1)}, bf16[8,1,4098]{2,0,1:T(8,128)(2,1)S(1)}, u32[]{:S(2)}, u32[]{:S(2)}) collective-permute-start(bf16[8,1,4098]{2,0,1:T(8,128)(2,1)S(1)} %get-tuple-element.6), channel_id=1, source_target_pairs={{1,0},{2,1},{3,2},{4,3},{5,4},{6,5},{7,6},{8,7},{9,8},{10,9},{11,1... | collective-permute-start | bytes 196712 | tf_op jit(solution)/shard_map/ppermute | solution.py:21
where the time goes:
time: 506 us; the launch traced here: 504 us
  other arithmetic  246 us (49%)
  local copies, waits for them, and re-layouts  97.5 us (19%)
  blocking collectives  85.5 us (17%)
  starting transfers between devices  38.7 us (8%)
  waiting for transfers between devices  23.4 us (5%)
  matrix products  11.9 us (2%)
    unnamed x2, other arithmetic  186 us
    all_to_all x1, blocking collectives, body(): lax.all_to_all(aligned_strip, 'xy', split_axis=1, concat_axis=2, tiled=True)  60.3 us
    all_to_all x2, local copies, waits for them, and re-layouts, body(): lax.all_to_all(lax.all_to_all(aligned_strip, 'xy', split_axis=1, concat_a...  29.7 us
    convert_element_type x1, other arithmetic, body(): return (second + group_data.astype(jnp.float32)).astype(jnp.bfloat16)  27.6 us
    convert_element_type x1, other arithmetic, body(): first_pass = jnp.maximum(stencil(pad_sections(rim_one.astype(jnp.float32)...  27.6 us
    unnamed x25, local copies, waits for them, and re-layouts  25.9 us
    all_to_all x1, blocking collectives, body(): lax.all_to_all(lax.all_to_all(aligned_strip, 'xy', split_axis=1, concat_a...  25.2 us
    all_to_all x2, local copies, waits for them, and re-layouts, body(): lax.all_to_all(aligned_strip, 'xy', split_axis=1, concat_axis=2, tiled=True)  25.1 us
  transfers between devices with their start and end apart: 10, of which 5 were waited for; matrix products, arithmetic and copies ran while one was open for 2% of the time, Pallas kernels for 0%

commit v1 on v0

--- a/solution.py
+++ b/solution.py
@@ -82,7 +82,12 @@
     ).astype(jnp.bfloat16)
     aligned_strip = warped.reshape(sections_dev, width, edge)
     group_data = lax.all_to_all(
-        lax.all_to_all(aligned_strip, "xy", split_axis=1, concat_axis=2, tiled=True),
+        jnp.concatenate(
+            lax.all_to_all(
+                jnp.stack(jnp.split(aligned_strip, lax.axis_size("xy"), axis=1)), "xy", 0, 0
+            ),
+            axis=2,
+        ),
         "sec",
         split_axis=2,
         concat_axis=0,

time: 506 us -> 496 us (0.980)
  other arithmetic: 246 us -> 239 us
    all_to_all x4 -> x2, local copies, waits for them, and re-layouts: 54.8 us -> 29.7 us  [body(): lax.all_to_all(jnp.concatenate(lax.all_to_all(jnp.stack(jnp.split(aligned...]
    reshape x1 -> x2, local copies, waits for them, and re-layouts: 1.62 us -> 25.1 us  [body(): jnp.concatenate(lax.all_to_all(jnp.stack(jnp.split(aligned_strip, lax.axi...]
    unnamed x2 -> x1, other arithmetic: 186 us -> 179 us
    unnamed x25 -> x85, local copies, waits for them, and re-layouts: 25.9 us -> 24 us
where the time goes in v1:
time: 496 us; the launch traced here: 494 us
  other arithmetic  239 us (48%)
  local copies, waits for them, and re-layouts  94.1 us (19%)
  blocking collectives  85.5 us (17%)
  starting transfers between devices  38.7 us (8%)
  waiting for transfers between devices  23.5 us (5%)
  matrix products  11.9 us (2%)
    unnamed x1, other arithmetic  179 us
    all_to_all x1, blocking collectives, body(): lax.all_to_all(jnp.stack(jnp.split(aligned_strip, lax.axis_size('xy'), ax...  60.3 us
    all_to_all x2, local copies, waits for them, and re-layouts, body(): lax.all_to_all(jnp.concatenate(lax.all_to_all(jnp.stack(jnp.split(aligned...  29.7 us
    convert_element_type x1, other arithmetic, body(): return (second + group_data.astype(jnp.float32)).astype(jnp.bfloat16)  27.7 us
    convert_element_type x1, other arithmetic, body(): first_pass = jnp.maximum(stencil(pad_sections(rim_one.astype(jnp.float32)...  27.6 us
    all_to_all x1, blocking collectives, body(): lax.all_to_all(jnp.concatenate(lax.all_to_all(jnp.stack(jnp.split(aligned...  25.3 us
    reshape x2, local copies, waits for them, and re-layouts, body(): jnp.concatenate(lax.all_to_all(jnp.stack(jnp.split(aligned_strip, lax.axi...  25.1 us
    unnamed x85, local copies, waits for them, and re-layouts  24 us
  transfers between devices with their start and end apart: 10, of which 5 were waited for; matrix products, arithmetic and copies ran while one was open for 2% of the time, Pallas kernels for 0%

profile of v1, /device:TPU:9, one launch (start us, length us, event | category | flops | bytes accessed | tf_op | source)
XLA Modules:
  0.0 493.9 jit_solution(16365179551710661039)
XLA Ops:
  0.0 3.7 collective-permute-start
  3.7 9.4 %collective-permute-start.1 = (bf16[1,512,1024]{2,1,0:T(8,128)(2,1)}, bf16[1,512,1024]{2,1,0:T(8,128)(2,1)S(1)}, u32[]{:S(2)}, u32[]{:S(2)}) collective-permute-start(bf16[1,512,1024]{2,1,0:T(8,128)(2,1)} %param.5), channel_id=1, source_target_pairs={{1,0},{2,1},{3,2},{4,3},{5,4},{6,5},{7,6},{8,7},{9,8},{10,9},{11,1... | collective-permute-start | bytes 3145736 | tf_op jit(solution)/shard_map/ppermute | solution.py:10
  13.1 0.9 fusion.109
  14.0 1.8 stack.208
  15.8 1.0 fusion.111
  16.8 0.0 copy-done.8
  16.8 0.1 iota_compare_fusion.1
  16.9 0.1 fusion.122
  16.9 0.0 copy-done.7
  17.0 17.3 %collective-permute-done = bf16[1,512,1024]{2,1,0:T(8,128)(2,1)S(1)} collective-permute-done((bf16[1,512,1024]{2,1,0:T(8,128)(2,1)}, bf16[1,512,1024]{2,1,0:T(8,128)(2,1)S(1)}, u32[]{:S(2)}, u32[]{:S(2)}) %collective-permute-start) | collective-permute-done | bytes 1048608 | tf_op jit(solution)/shard_map/ppermute | solution.py:10
  34.2 1.6 stack.207
  35.8 0.0 collective-permute-done.1
  35.8 0.8 stack.209
  36.6 0.0 copy-start.2
  36.6 0.0 copy-start.3
  36.6 0.0 copy-start.4
  36.6 8.0 %bitcast_convert_fusion = bf16[2,512,512]{2,0,1:T(2,128)(2,1)} fusion(bf16[1,1,512,2,512]{4,3,0,2,1:T(2,128)(2,1)S(1)} %stack.209, bf16[1,1,512,2,512]{4,3,0,2,1:T(2,128)(2,1)S(1)} %stack.208, bf16[1,1,512,2,512]{4,3,0,2,1:T(2,128)(2,1)} %stack.207, pred[3,2,2]{2,0,1:T(4,128)(4,1)S(1)} %fusion.122), kind=kOutput, calls=%fused_computation.148 | convolution fusion | flops 16252928 | bytes 4194316 | tf_op jit(solution)/shard_map/ksnm,ksimj->snij/dot_general | solution.py:72
  44.6 0.0 copy-done.2
  44.6 0.0 copy-done.3
  44.6 0.0 copy-done.4
  44.6 3.9 convolution_convert_fusion
  49.3 60.3 %all_to_all.23 = bf16[64,1,16,512]{3,2,1,0:T(8,128)(2,1)S(1)} all-to-all(bf16[64,1,16,512]{3,2,1,0:T(8,128)(2,1)S(1)} %constant_dynamic-update-slice_fusion), channel_id=1, replica_groups=mesh['sec'=8,'xy'=64] {'xy'}, dimensions={0} | all-to-all | bytes 2097152 | tf_op jit(solution)/shard_map/all_to_all | solution.py:86
  109.5 0.1 copy.81
  109.6 25.1 %copy.77 = bf16[1,16,32768]{1,0,2:T(2,128)(2,1)} copy(bf16[1,16,32768]{2,1,0:T(8,128)(2,1)S(1)} %bitcast.422) | data formatting | bytes 2097152 | tf_op jit(solution)/shard_map/reshape | solution.py:85
  134.7 0.5 broadcast.323
  135.2 179.2 %reduce = bf16[32768,16]{1,0:T(8,128)(2,1)} reduce(bf16[32768,1,16]{2,1,0:T(2,128)(2,1)} %bitcast.418, bf16[]{:T(256)} %broadcast.323), dimensions={1}, to_apply=%bitcast.414.reduce_sub_computation | reduce | bytes 2097154
  314.4 10.4 %reshape.325 = bf16[8,2,32768]{2,1,0:T(2,128)(2,1)S(1)} reshape(bf16[32768,16]{1,0:T(8,128)(2,1)} %reduce) | data formatting | bytes 2097152
  324.8 25.3 %all_to_all.24 = bf16[8,2,32768]{2,1,0:T(2,128)(2,1)S(1)} all-to-all(bf16[8,2,32768]{2,1,0:T(2,128)(2,1)S(1)} %reshape.325), channel_id=1, replica_groups=mesh['sec'=8,'xy'=64] {'sec'}, dimensions={0} | all-to-all | bytes 2097152 | tf_op jit(solution)/shard_map/all_to_all | solution.py:84
  350.1 12.3 %reshape.326 = bf16[32768,1,16]{2,1,0:T(2,128)(2,1)} reshape(bf16[8,2,32768]{2,1,0:T(2,128)(2,1)S(1)} %all_to_all.24) | data formatting | bytes 2097152
  362.4 29.6 %copy.78 = bf16[1,16,32768]{2,1,0:T(8,128)(2,1)S(1)} copy(bf16[1,16,32768]{1,0,2:T(2,128)(2,1)} %bitcast.419) | data formatting | bytes 2097152 | tf_op jit(solution)/shard_map/all_to_all | solution.py:84
  392.0 0.0 copy-start.5
  392.0 0.6 copy.82
  392.6 0.1 bitcast_bitcast_fusion
  392.7 0.1 fusion.143
  392.8 3.1 collective-permute-start.2
  395.9 1.9 collective-permute-start.3
  397.8 0.7 fusion.146
  398.5 0.0 collective-permute-done.2
  398.6 2.6 collective-permute-done.3
  401.1 1.6 concatenate.13
  402.7 0.0 copy-start
  402.7 3.0 collective-permute-start.4
  405.8 4.6 collective-permute-start.5
  410.4 0.7 fusion.147
  411.0 0.0 collective-permute-done.4
  411.1 0.4 collective-permute-done.5
  411.5 1.4 maximum_convert_fusion
  412.9 0.0 copy-start.6
  412.9 27.6 %fusion.43 = bf16[8,16,4096]{2,0,1:T(8,128)(2,1)} fusion(f32[8,18,4098]{2,0,1:T(8,128)S(1)} %maximum_convert_fusion, f32[]{:T(128)} %bitcast.105, f32[]{:T(128)} %bitcast.104, f32[]{:T(128)} %bitcast.103, f32[]{:T(128)} %bitcast.102, f32[]{:T(128)} %bitcast.101, f32[]{:T(128)} %bitcast.100, f32[]{:T(128)} %bitcast.99, f32[]{:T(128)} %bitcast.98, ...), kind=kLoop, calls=%fused_computation.80 | loop fusion | flops 28835840 | bytes 22356076 | tf_op jit(solution)/shard_map/convert_element_type | solution.py:107
  440.6 0.9 fusion.142
  441.4 3.0 collective-permute-start.6
  444.5 1.9 collective-permute-start.7
  446.4 0.7 fusion.144
  447.1 0.0 collective-permute-done.6
  447.1 2.6 collective-permute-done.7
  449.7 2.9 concatenate.15
  452.6 2.3 collective-permute-start.8
  454.9 5.7 %collective-permute-start.9 = (bf16[8,1,4098]{2,0,1:T(8,128)(2,1)S(1)}, bf16[8,1,4098]{2,0,1:T(8,128)(2,1)S(1)}, u32[]{:S(2)}, u32[]{:S(2)}) collective-permute-start(bf16[8,1,4098]{2,0,1:T(8,128)(2,1)S(1)} %get-tuple-element.6), channel_id=1, source_target_pairs={{1,0},{2,1},{3,2},{4,3},{5,4},{6,5},{7,6},{8,7},{9,8},{10,9},{11,1... | collective-permute-start | bytes 196712 | tf_op jit(solution)/shard_map/ppermute | solution.py:21
  460.6 0.7 fusion.145
  461.3 0.0 collective-permute-done.8
  461.3 0.6 collective-permute-done.9
  462.0 1.4 maximum_convert_fusion.1
  463.4 27.7 %fusion.89 = bf16[8,16,4096]{2,0,1:T(8,128)(2,1)} fusion(f32[8,18,4098]{2,0,1:T(8,128)S(1)} %maximum_convert_fusion.1, f32[]{:T(128)} %bitcast.131, f32[]{:T(128)} %bitcast.130, f32[]{:T(128)} %bitcast.129, f32[]{:T(128)} %bitcast.128, f32[]{:T(128)} %bitcast.127, f32[]{:T(128)} %bitcast.126, f32[]{:T(128)} %bitcast.125, f32[]{:T(128)} %bitcast.124, ...), kind=kLoop, calls=%fused_computation.126 | loop fusion | flops 29360128 | bytes 23404652 | tf_op jit(solution)/shard_map/convert_element_type | solution.py:112
  491.1 2.8 copy.79
  (75 shorter events, 0.3 us)
Async XLA Ops:
  0.0 16.8 %copy-start.8 = (s32[1,2,2]{2,1,0:T(2,128)S(1)}, s32[1,2,2]{2,1,0:T(2,128)}, u32[]{:S(2)}) copy-start(s32[1,2,2]{2,1,0:T(2,128)} %param.6) | copy-start | bytes 52
  0.0 16.9 %copy-start.7 = (f32[1,2,2]{2,1,0:T(2,128)S(1)}, f32[1,2,2]{2,1,0:T(2,128)}, u32[]{:S(2)}) copy-start(f32[1,2,2]{2,1,0:T(2,128)} %param.7) | copy-start | bytes 52
  0.0 34.2 %collective-permute-start = (bf16[1,512,1024]{2,1,0:T(8,128)(2,1)}, bf16[1,512,1024]{2,1,0:T(8,128)(2,1)S(1)}, u32[]{:S(2)}, u32[]{:S(2)}) collective-permute-start(bf16[1,512,1024]{2,1,0:T(8,128)(2,1)} %param.5), channel_id=1, source_target_pairs={{0,1},{1,2},{2,3},{3,4},{4,5},{5,6},{6,7},{7,8},{8,9},{9,10},{10,1... | collective-permute-start | bytes 3145736 | tf_op jit(solution)/shard_map/ppermute | solution.py:10
  3.7 32.1 %collective-permute-start.1 = (bf16[1,512,1024]{2,1,0:T(8,128)(2,1)}, bf16[1,512,1024]{2,1,0:T(8,128)(2,1)S(1)}, u32[]{:S(2)}, u32[]{:S(2)}) collective-permute-start(bf16[1,512,1024]{2,1,0:T(8,128)(2,1)} %param.5), channel_id=1, source_target_pairs={{1,0},{2,1},{3,2},{4,3},{5,4},{6,5},{7,6},{8,7},{9,8},{10,9},{11,1... | collective-permute-start | bytes 3145736 | tf_op jit(solution)/shard_map/ppermute | solution.py:10
  36.6 8.0 %copy-start.2 = (pred[512,512]{1,0:T(8,128)(4,1)S(1)}, pred[512,512]{1,0:T(8,128)(4,1)}, u32[]{:S(2)}) copy-start(pred[512,512]{1,0:T(8,128)(4,1)} %get-tuple-element.78) | copy-start | bytes 786436
  36.6 8.0 %copy-start.3 = (pred[512,512]{1,0:T(8,128)(4,1)S(1)}, pred[512,512]{1,0:T(8,128)(4,1)}, u32[]{:S(2)}) copy-start(pred[512,512]{1,0:T(8,128)(4,1)} %get-tuple-element.79) | copy-start | bytes 786436
  36.6 8.0 %copy-start.4 = (pred[512,512]{1,0:T(8,128)(4,1)S(1)}, pred[512,512]{1,0:T(8,128)(4,1)}, u32[]{:S(2)}) copy-start(pred[512,512]{1,0:T(8,128)(4,1)} %get-tuple-element.80) | copy-start | bytes 786436
  392.0 5.8 %copy-start.5 = (f32[3,3,3]{2,1,0:T(4,128)S(1)}, f32[3,3,3]{2,1,0:T(4,128)}, u32[]{:S(2)}) copy-start(f32[3,3,3]{2,1,0:T(4,128)} %param.8) | copy-start | bytes 328
  392.8 5.8 %collective-permute-start.2 = (bf16[8,16,1]{2,0,1:T(8,128)(2,1)S(1)}, bf16[8,16,1]{2,0,1:T(8,128)(2,1)S(1)}, u32[]{:S(2)}, u32[]{:S(2)}) collective-permute-start(bf16[8,16,1]{2,0,1:T(8,128)(2,1)S(1)} %get-tuple-element.12), channel_id=1, source_target_pairs={{0,64},{64,128},{128,192},{192,256},{256,320},{320,384},{384,448},... | collective-permute-start | bytes 776 | tf_op jit(solution)/shard_map/ppermute | solution.py:20
  395.9 5.2 %collective-permute-start.3 = (bf16[8,16,1]{2,0,1:T(8,128)(2,1)S(1)}, bf16[8,16,1]{2,0,1:T(8,128)(2,1)S(1)}, u32[]{:S(2)}, u32[]{:S(2)}) collective-permute-start(bf16[8,16,1]{2,0,1:T(8,128)(2,1)S(1)} %get-tuple-element.11), channel_id=1, source_target_pairs={{64,0},{128,64},{192,128},{256,192},{320,256},{384,320},{448,384},... | collective-permute-start | bytes 776 | tf_op jit(solution)/shard_map/ppermute | solution.py:21
  402.7 8.3 %copy-start = (bf16[8,16,4098]{2,0,1:T(8,128)(2,1)}, bf16[8,16,4098]{2,0,1:T(8,128)(2,1)S(1)}, u32[]{:S(2)}) copy-start(bf16[8,16,4098]{2,0,1:T(8,128)(2,1)S(1)} %concatenate.13) | copy-start | bytes 3147268
  402.7 8.3 %collective-permute-start.4 = (bf16[8,1,4098]{2,0,1:T(8,128)(2,1)S(1)}, bf16[8,1,4098]{2,0,1:T(8,128)(2,1)S(1)}, u32[]{:S(2)}, u32[]{:S(2)}) collective-permute-start(bf16[8,1,4098]{2,0,1:T(8,128)(2,1)S(1)} %get-tuple-element.7), channel_id=1, source_target_pairs={{0,1},{1,2},{2,3},{3,4},{4,5},{5,6},{6,7},{7,8},{8,9},{9,10},{10,1... | collective-permute-start | bytes 196712 | tf_op jit(solution)/shard_map/ppermute | solution.py:20
  405.8 5.7 %collective-permute-start.5 = (bf16[8,1,4098]{2,0,1:T(8,128)(2,1)S(1)}, bf16[8,1,4098]{2,0,1:T(8,128)(2,1)S(1)}, u32[]{:S(2)}, u32[]{:S(2)}) collective-permute-start(bf16[8,1,4098]{2,0,1:T(8,128)(2,1)S(1)} %get-tuple-element.8), channel_id=1, source_target_pairs={{1,0},{2,1},{3,2},{4,3},{5,4},{6,5},{7,6},{8,7},{9,8},{10,9},{11,1... | collective-permute-start | bytes 196712 | tf_op jit(solution)/shard_map/ppermute | solution.py:21
  412.9 33.5 %copy-start.6 = (f32[3,3,3]{2,1,0:T(4,128)S(1)}, f32[3,3,3]{2,1,0:T(4,128)}, u32[]{:S(2)}) copy-start(f32[3,3,3]{2,1,0:T(4,128)} %param.9) | copy-start | bytes 328
  441.4 5.7 %collective-permute-start.6 = (bf16[8,16,1]{2,0,1:T(8,128)(2,1)S(1)}, bf16[8,16,1]{2,0,1:T(8,128)(2,1)S(1)}, u32[]{:S(2)}, u32[]{:S(2)}) collective-permute-start(bf16[8,16,1]{2,0,1:T(8,128)(2,1)S(1)} %get-tuple-element.10), channel_id=1, source_target_pairs={{0,64},{64,128},{128,192},{192,256},{256,320},{320,384},{384,448},... | collective-permute-start | bytes 776 | tf_op jit(solution)/shard_map/ppermute | solution.py:20
  444.5 5.2 %collective-permute-start.7 = (bf16[8,16,1]{2,0,1:T(8,128)(2,1)S(1)}, bf16[8,16,1]{2,0,1:T(8,128)(2,1)S(1)}, u32[]{:S(2)}, u32[]{:S(2)}) collective-permute-start(bf16[8,16,1]{2,0,1:T(8,128)(2,1)S(1)} %get-tuple-element.9), channel_id=1, source_target_pairs={{64,0},{128,64},{192,128},{256,192},{320,256},{384,320},{448,384},... | collective-permute-start | bytes 776 | tf_op jit(solution)/shard_map/ppermute | solution.py:21
  452.6 8.7 %copy-start.1 = (bf16[8,16,4098]{2,0,1:T(8,128)(2,1)}, bf16[8,16,4098]{2,0,1:T(8,128)(2,1)S(1)}, u32[]{:S(2)}) copy-start(bf16[8,16,4098]{2,0,1:T(8,128)(2,1)S(1)} %concatenate.15) | copy-start | bytes 3147268
  452.6 8.7 %collective-permute-start.8 = (bf16[8,1,4098]{2,0,1:T(8,128)(2,1)S(1)}, bf16[8,1,4098]{2,0,1:T(8,128)(2,1)S(1)}, u32[]{:S(2)}, u32[]{:S(2)}) collective-permute-start(bf16[8,1,4098]{2,0,1:T(8,128)(2,1)S(1)} %get-tuple-element.5), channel_id=1, source_target_pairs={{0,1},{1,2},{2,3},{3,4},{4,5},{5,6},{6,7},{7,8},{8,9},{9,10},{10,1... | collective-permute-start | bytes 196712 | tf_op jit(solution)/shard_map/ppermute | solution.py:20
  454.9 7.0 %collective-permute-start.9 = (bf16[8,1,4098]{2,0,1:T(8,128)(2,1)S(1)}, bf16[8,1,4098]{2,0,1:T(8,128)(2,1)S(1)}, u32[]{:S(2)}, u32[]{:S(2)}) collective-permute-start(bf16[8,1,4098]{2,0,1:T(8,128)(2,1)S(1)} %get-tuple-element.6), channel_id=1, source_target_pairs={{1,0},{2,1},{3,2},{4,3},{5,4},{6,5},{7,6},{8,7},{9,8},{10,9},{11,1... | collective-permute-start | bytes 196712 | tf_op jit(solution)/shard_map/ppermute | solution.py:21
